TPU v7x, 32 devices: a whole 2x2x4 slice. The times are simulated.
32 devices in a mesh: blk: 8 (over y, x, core), cross: 4 (over z).
Axes of the slice: x: 2, y: 2, z: 4, core: 2. Of those that a mesh axis runs over, the one named last changes fastest.
Arguments:
- receiver_spectra: float32 [4096, 2, 1024], P(('blk', 'cross')), may hold values from -400 to 400
- source_spectra: float32 [4096, 2, 1024], P(('blk', 'cross')), may hold values from -400 to 400
- quality: int32 [4096], P(('blk', 'cross')), may hold values 0 or 1
- slot_order: int32 [32, 128], P(('blk', 'cross')), may hold values from 0 to 127, each once within a row
- owners: int32 [2, 8], replicated, may hold values from 0 to 3
Outputs:
- correlations: bfloat16 [2, 8, 4, 128, 128, 256], P(None, 'blk', 'cross')
Inputs may be any that keep to these rules, and one draw needn't show every extreme that they name: `slot_order`: each row is a permutation of 0 to 127.
All inputs are finite; a program needn't handle non-finite values. No bound on the sum of `quality` on one device may be relied on, other than what follows from the above.
Results may differ from a plain program's by a relative error of at most 0.0056.
Values sent between devices are 32-bit elements; how exact they have to be, the bound alone decides.
A program may use at most 128 MiB of HBM per device.

v0:
```python
import math
import jax
import jax.numpy as jnp
from jax import lax
from jax.sharding import PartitionSpec as P

L = 256
STEPS = 2


def passed_along(value, axis, steps):
    count = lax.axis_size(axis)
    pairs = [(source, (source + steps) % count) for source in range(count)]
    return lax.ppermute(value, axis, pairs)


def lag_tables(bins, lags):
    bin_index = jnp.arange(bins, dtype=jnp.int32)
    odd_index = 2 * jnp.arange(lags // 2, dtype=jnp.int32) + 1
    phase_turns = jnp.mod(bin_index[:, None] * odd_index[None, :], 4 * bins).astype(jnp.float32)
    phase_angle = phase_turns * (math.pi / (2 * bins))
    cos_table = (jnp.cos(phase_angle) / bins).astype(jnp.bfloat16)
    sin_table = (-jnp.sin(phase_angle) / bins).astype(jnp.bfloat16)
    return (cos_table, sin_table)


def whiten(spectra):
    mean_power = jnp.mean(spectra * spectra, axis=(1, 2), keepdims=True)
    return spectra * lax.rsqrt(mean_power + 1e-06)


def correlate(panel_spec, slab_spec, cos_table, sin_table):
    npanel = panel_spec.shape[0]
    nslab = slab_spec.shape[0]
    width = math.gcd(npanel, 16)
    blocks = panel_spec.reshape(npanel // width, width, 2, panel_spec.shape[2])

    def one_block(source):
        inphase = (
            source[:, None, 0, :] * slab_spec[None, :, 0, :]
            + source[:, None, 1, :] * slab_spec[None, :, 1, :]
        )
        quadrature = (
            source[:, None, 1, :] * slab_spec[None, :, 0, :]
            - source[:, None, 0, :] * slab_spec[None, :, 1, :]
        )
        inphase = inphase.astype(jnp.bfloat16).reshape(width * nslab, -1)
        quadrature = quadrature.astype(jnp.bfloat16).reshape(width * nslab, -1)
        even = jnp.dot(inphase, cos_table, preferred_element_type=jnp.float32)
        odd = jnp.dot(quadrature, sin_table, preferred_element_type=jnp.float32)
        joined = jnp.concatenate([even + odd, even - odd], axis=-1).astype(jnp.bfloat16)
        return joined.reshape(width, nslab, -1)

    lagged = lax.map(one_block, blocks)
    return lagged.reshape(npanel, nslab, lagged.shape[-1])


def local(receiver_spectra, source_spectra, quality, slot_order, owners):
    bins = receiver_spectra.shape[2]
    npanel = source_spectra.shape[0]
    cos_table, sin_table = lag_tables(bins, L)
    kept = quality.astype(jnp.float32)[:, None, None]
    receivers = whiten(receiver_spectra) * kept
    receivers = jnp.take(receivers, slot_order[0], axis=0)
    sources = whiten(source_spectra)
    block_index = lax.axis_index("blk")
    my_owners = lax.dynamic_index_in_dim(owners, block_index, 1, keepdims=False)
    every_panel = lax.all_gather(sources, "cross", axis=0, tiled=True)
    moving = receivers
    results = []
    for loop_step in range(STEPS):
        if loop_step > 0:
            moving = passed_along(moving, "blk", 1)
        owner_index = my_owners[loop_step]
        panel_spec = lax.dynamic_slice_in_dim(every_panel, owner_index * npanel, npanel, 0)
        results.append(correlate(panel_spec, moving, cos_table, sin_table))
    return jnp.stack(results)[:, None, None]


def solution(mesh):
    placed = (
        P(("blk", "cross"), None, None),
        P(("blk", "cross"), None, None),
        P(("blk", "cross")),
        P(("blk", "cross"), None),
        P(),
    )
    return jax.shard_map(
        local,
        mesh=mesh,
        in_specs=placed,
        out_specs=P(None, "blk", "cross", None, None, None),
        check_vma=False,
    )
```

profile of v0, /device:TPU:0, one launch (start us, length us, event | category | flops | bytes accessed | tf_op | source)
XLA Modules:
  0.0 305.8 jit_solution(16467009084390342149)
XLA Ops:
  21.7 73.5 %all-gather.2.cloned.1.call-done = f32[512,2,1024]{2,1,0:T(2,128)} async-done(((f32[128,2,1024]{2,1,0:T(2,128)}), f32[512,2,1024]{2,1,0:T(2,128)}) %all-gather.2.cloned.1.call-update) | async-done | bytes 4194320 | tf_op jit(solution)/shard_map/all_gather | solution.py:68
  95.1 3.2 %constant_dynamic-slice_fusion.1 = (f32[128,2,1024]{2,1,0:T(2,128)S(1)}, f32[128,2,1024]{2,1,0:T(2,128)}) fusion(f32[512,2,1024]{2,1,0:T(2,128)} %all-gather.2.cloned.1.call-done, s32[]{:T(128)S(6)} %select_n.44, s32[]{:T(128)S(6)} %select_n.49), kind=kLoop, calls=%fused_computation.86 | loop fusion | bytes 4194312 | tf_op jit(solution)/shard_map/dynamic_slice | solution.py:75
  98.4 4.3 %broadcast.91.clone = bf16[8,16,128,256]{3,2,1,0:T(8,128)(2,1)} broadcast(bf16[]{:T(256)} %constant.66.clone.1), dimensions={} | broadcast | bytes 8388610 | tf_op jit(solution)/shard_map/broadcast.6
  102.6 92.7 %while.25 = (s32[]{:T(128)}, bf16[8,16,128,256]{3,2,1,0:T(8,128)(2,1)}, f32[8,16,2,1024]{3,2,1,0:T(2,128)}, f32[128,2,1024]{2,1,0:T(2,128)S(1)}, s32[128]{0:T(128)S(1)}, /*index=5*/s32[]{:T(128)}) while((s32[]{:T(128)}, bf16[8,16,128,256]{3,2,1,0:T(8,128)(2,1)}, f32[8,16,2,1024]{3,2,1,0:T(2,128)}, ...), condition=%wide.region_5.6_spmd.clone.clone, body=%wide.region_4.5_spmd.clone.clone.sunk | while | flops 1097990144 | bytes 28181588 | solution.py:54
  107.4 2.9 fusion.81
  110.3 2.8 add_convert_fusion.7
  119.0 2.9 fusion.81
  130.6 2.9 fusion.81
  142.1 2.9 fusion.81
  153.7 2.9 fusion.81
  165.3 2.9 fusion.81
  176.9 2.9 fusion.81
  188.5 2.9 fusion.81
  195.4 4.3 %broadcast.91.clone.1 = bf16[8,16,128,256]{3,2,1,0:T(8,128)(2,1)} broadcast(bf16[]{:T(256)} %constant.66.clone.1), dimensions={} | broadcast | bytes 8388610 | tf_op jit(solution)/shard_map/broadcast.6
  199.7 85.5 %while.24 = (s32[]{:T(128)}, bf16[8,16,128,256]{3,2,1,0:T(8,128)(2,1)}, f32[8,16,2,1024]{3,2,1,0:T(2,128)S(1)}, f32[128,2,1024]{2,1,0:T(2,128)S(1)}, s32[128]{0:T(128)S(1)}, /*index=5*/s32[]{:T(128)}) while((s32[]{:T(128)}, bf16[8,16,128,256]{3,2,1,0:T(8,128)(2,1)}, f32[8,16,2,1024]{3,2,1,0:T(2,128)S(1)}, ...), condition=%wide.region_3.4_spmd.clone.clone, body=%wide.region_2.3_spmd.clone.clone.sunk | while | flops 1097990144 | bytes 28181588 | solution.py:54
  203.5 2.9 fusion.76
  214.3 2.9 fusion.76
  224.9 2.9 fusion.76
  235.6 2.9 fusion.76
  246.3 2.9 fusion.76
  257.0 2.9 fusion.76
  267.7 2.9 fusion.76
  278.4 2.9 fusion.76
  285.2 13.8 %maximum_bitcast_fusion = bf16[2,1,1,128,128,256]{5,4,3,2,1,0:T(8,128)(2,1)} fusion(bf16[1,128,128,256]{3,2,1,0:T(8,128)(2,1)} %bitcast.87, bf16[1,128,128,256]{3,2,1,0:T(8,128)(2,1)} %bitcast.86), kind=kLoop, calls=%fused_computation.75 | loop fusion | flops 8388608 | bytes 33554432 | tf_op jit(solution)/shard_map/broadcast_in_dim | solution.py:77
  (152 shorter events, 142.6 us)
Async XLA Ops:
  6.5 13.2 %copy-start = (s32[2,8]{1,0:T(2,128)S(1)}, s32[2,8]{1,0:T(2,128)}, u32[]{:S(2)}) copy-start(s32[2,8]{1,0:T(2,128)} %param.13) | copy-start | bytes 196
  6.5 11.9 %copy-start.2 = (s32[1,128]{1,0:T(1,128)S(1)}, s32[1,128]{1,0:T(1,128)}, u32[]{:S(2)}) copy-start(s32[1,128]{1,0:T(1,128)} %param.12) | copy-start | bytes 1540
  6.5 88.6 %all-gather.2.cloned.1.call-start = ((), (), s32[]{:S(2)}) async-start(), calls=%async_computation | async-start | bytes 5242880 | tf_op jit(solution)/shard_map/all_gather | solution.py:68
  19.0 79.3 %collective-permute-start = (f32[128,2,1024]{2,1,0:T(2,128)S(1)}, f32[128,2,1024]{2,1,0:T(2,128)S(1)}, u32[]{:S(2)}, u32[]{:S(2)}) collective-permute-start(f32[128,2,1024]{2,1,0:T(2,128)S(1)} %broadcast_select_fusion), channel_id=1, source_target_pairs={{0,4},{4,8},{8,12},{12,16},{16,20},{20,24},{24,28},{28,0},{1,5},{5... | collective-permute-start | bytes 3145736 | tf_op jit(solution)/shard_map/ppermute | solution.py:14
  285.2 13.8 %copy-start.1 = (s32[2,8]{1,0:T(2,128)S(1)}, s32[2,8]{1,0:T(2,128)}, u32[]{:S(2)}) copy-start(s32[2,8]{1,0:T(2,128)} %param.13) | copy-start | bytes 196
Sparse Core Ops, SparseCore 0:
  11.6 83.4 all-gather.1
where the time goes:
time: 306 us
  matrix products  90.8 us (30%)
  other arithmetic  85.6 us (28%)
  waiting for transfers between devices  73.5 us (24%)
  local copies, waits for them, and re-layouts  39.7 us (13%)
  between operations  14.7 us (5%)
    all_gather x1, waiting for transfers between devices, local(): every_panel = lax.all_gather(sources, 'cross', axis=0, tiled=True)  73.5 us
    dot_general x16, matrix products, one_block(): odd = jnp.dot(quadrature, sin_table, preferred_element_type=jnp.float32)  45.8 us
    dot_general x16, matrix products, one_block(): even = jnp.dot(inphase, cos_table, preferred_element_type=jnp.float32)  45 us
    convert_element_type x16, other arithmetic, one_block(): quadrature = quadrature.astype(jnp.bfloat16).reshape(width * nslab, -1)  42.7 us
    dynamic_update_slice x16, other arithmetic, correlate(): lagged = lax.map(one_block, blocks)  18.4 us
    broadcast_in_dim x1, other arithmetic, local(): return jnp.stack(results)[:, None, None]  13.8 us
    slice x16, local copies, waits for them, and re-layouts, one_block(): slab_spec[None, :, 0, :]  13 us
    another operation x2, local copies, waits for them, and re-layouts  8.57 us
  transfers between devices with their start and end apart: 2, of which 1 were waited for; matrix products, arithmetic and copies ran while one was open for 4% of the time, Pallas kernels for 0%

commit v1 on v0

--- a/solution.py
+++ b/solution.py
@@ -65,7 +65,14 @@
     sources = whiten(source_spectra)
     block_index = lax.axis_index("blk")
     my_owners = lax.dynamic_index_in_dim(owners, block_index, 1, keepdims=False)
-    every_panel = lax.all_gather(sources, "cross", axis=0, tiled=True)
+    ring = [sources]
+    for hop in range(3):
+        ring.append(lax.ppermute(ring[-1], "cross", [(dev, (dev + 1) % 4) for dev in range(4)]))
+    every_panel = jnp.roll(
+        jnp.concatenate(ring[::-1], axis=0),
+        (lax.axis_index("cross") + 1) * ring[0].shape[0],
+        axis=0,
+    )
     moving = receivers
     results = []
     for loop_step in range(STEPS):

time: 306 us -> 295 us (0.964)
  between operations: 14.7 us -> 1.37 us
  waiting for transfers between devices: 73.5 us -> 65.1 us
  local copies, waits for them, and re-layouts: 39.7 us -> 46.3 us
    all_gather x1 -> x0, waiting for transfers between devices: 73.5 us -> none  [local(): every_panel = lax.all_gather(sources, 'cross', axis=0, tiled=True)]
    ppermute x0 -> x3, waiting for transfers between devices: none -> 65.1 us  [local(): lax.ppermute(ring[-1], 'cross', [(dev, (dev + 1) % 4) for dev in range(4)])]
    unnamed x6 -> x18, local copies, waits for them, and re-layouts: 0.01 us -> 6.9 us
    ppermute x0 -> x3, starting transfers between devices: none -> 3.11 us  [local(): lax.ppermute(ring[-1], 'cross', [(dev, (dev + 1) % 4) for dev in range(4)])]
  transfers between devices with their start and end apart: 2 -> 4, of which waited for: 1 -> 3; matrix products, arithmetic and copies ran while one was open for 4% -> 7% of each run, Pallas kernels for 0% -> 0%
where the time goes in v1:
time: 295 us
  matrix products  90.8 us (31%)
  other arithmetic  86.8 us (29%)
  waiting for transfers between devices  65.1 us (22%)
  local copies, waits for them, and re-layouts  46.3 us (16%)
  starting transfers between devices  3.35 us (1%)
    ppermute x3, waiting for transfers between devices, local(): lax.ppermute(ring[-1], 'cross', [(dev, (dev + 1) % 4) for dev in range(4)])  65.1 us
    dot_general x16, matrix products, one_block(): odd = jnp.dot(quadrature, sin_table, preferred_element_type=jnp.float32)  45.8 us
    dot_general x16, matrix products, one_block(): even = jnp.dot(inphase, cos_table, preferred_element_type=jnp.float32)  45 us
    convert_element_type x16, other arithmetic, one_block(): quadrature = quadrature.astype(jnp.bfloat16).reshape(width * nslab, -1)  42.7 us
    dynamic_update_slice x16, other arithmetic, correlate(): lagged = lax.map(one_block, blocks)  18.4 us
    broadcast_in_dim x1, other arithmetic, local(): return jnp.stack(results)[:, None, None]  13.8 us
    slice x16, local copies, waits for them, and re-layouts, one_block(): slab_spec[None, :, 0, :]  13 us
    another operation x2, local copies, waits for them, and re-layouts  8.56 us
  transfers between devices with their start and end apart: 4, of which 3 were waited for; matrix products, arithmetic and copies ran while one was open for 7% of the time, Pallas kernels for 0%

profile of v1, /device:TPU:0, one launch (start us, length us, event | category | flops | bytes accessed | tf_op | source)
XLA Modules:
  0.0 294.5 jit_solution(1800164442833819478)
XLA Ops:
  4.0 3.1 %collective-permute-start = (f32[128,2,1024]{2,1,0:T(2,128)S(1)}, f32[128,2,1024]{2,1,0:T(2,128)S(1)}, u32[]{:S(2)}, u32[]{:S(2)}) collective-permute-start(f32[128,2,1024]{2,1,0:T(2,128)S(1)} %broadcast_multiply_fusion), channel_id=1, source_target_pairs={{0,1},{1,2},{2,3},{3,0},{4,5},{5,6},{6,7},{7,4},{8,9},{9,10},{10,1... | collective-permute-start | bytes 3145736 | tf_op jit(solution)/shard_map/ppermute | solution.py:70
  7.1 25.2 %collective-permute-done = f32[128,2,1024]{2,1,0:T(2,128)S(1)} collective-permute-done((f32[128,2,1024]{2,1,0:T(2,128)S(1)}, f32[128,2,1024]{2,1,0:T(2,128)S(1)}, u32[]{:S(2)}, u32[]{:S(2)}) %collective-permute-start) | collective-permute-done | bytes 1048608 | tf_op jit(solution)/shard_map/ppermute | solution.py:70
  35.9 22.6 %collective-permute-done.1 = f32[128,2,1024]{2,1,0:T(2,128)} collective-permute-done((f32[128,2,1024]{2,1,0:T(2,128)S(1)}, f32[128,2,1024]{2,1,0:T(2,128)}, u32[]{:S(2)}, u32[]{:S(2)}) %collective-permute-start.1) | collective-permute-done | bytes 1048608 | tf_op jit(solution)/shard_map/ppermute | solution.py:70
  61.2 2.9 gather_fusion
  66.8 17.3 %collective-permute-done.2 = f32[128,2,1024]{2,1,0:T(2,128)} collective-permute-done((f32[128,2,1024]{2,1,0:T(2,128)}, f32[128,2,1024]{2,1,0:T(2,128)}, u32[]{:S(2)}, u32[]{:S(2)}) %collective-permute-start.2) | collective-permute-done | bytes 1048608 | tf_op jit(solution)/shard_map/ppermute | solution.py:70
  93.9 4.3 %broadcast.92.clone = bf16[8,16,128,256]{3,2,1,0:T(8,128)(2,1)} broadcast(bf16[]{:T(256)} %constant.113.clone.1), dimensions={} | broadcast | bytes 8388610 | tf_op jit(solution)/shard_map/broadcast.6
  98.1 92.7 %while.25 = (s32[]{:T(128)}, bf16[8,16,128,256]{3,2,1,0:T(8,128)(2,1)}, f32[8,16,2,1024]{3,2,1,0:T(2,128)}, f32[128,2,1024]{2,1,0:T(2,128)S(1)}, s32[128]{0:T(128)S(1)}, /*index=5*/s32[]{:T(128)}) while((s32[]{:T(128)}, bf16[8,16,128,256]{3,2,1,0:T(8,128)(2,1)}, f32[8,16,2,1024]{3,2,1,0:T(2,128)}, ...), condition=%wide.region_5.6_spmd.clone.clone, body=%wide.region_4.5_spmd.clone.clone.sunk | while | flops 1097990144 | bytes 28181588 | solution.py:54
  102.9 2.9 fusion.81
  114.5 2.9 fusion.81
  149.2 2.9 fusion.81
  160.8 2.9 fusion.81
  172.4 2.9 fusion.81
  184.0 2.9 fusion.81
  190.8 4.3 %broadcast.92.clone.1 = bf16[8,16,128,256]{3,2,1,0:T(8,128)(2,1)} broadcast(bf16[]{:T(256)} %constant.113.clone.1), dimensions={} | broadcast | bytes 8388610 | tf_op jit(solution)/shard_map/broadcast.6
  195.1 85.6 %while.24 = (s32[]{:T(128)}, bf16[8,16,128,256]{3,2,1,0:T(8,128)(2,1)}, f32[8,16,2,1024]{3,2,1,0:T(2,128)S(1)}, f32[128,2,1024]{2,1,0:T(2,128)S(1)}, s32[128]{0:T(128)S(1)}, /*index=5*/s32[]{:T(128)}) while((s32[]{:T(128)}, bf16[8,16,128,256]{3,2,1,0:T(8,128)(2,1)}, f32[8,16,2,1024]{3,2,1,0:T(2,128)S(1)}, ...), condition=%wide.region_3.4_spmd.clone.clone, body=%wide.region_2.3_spmd.clone.clone.sunk | while | flops 1097990144 | bytes 28181588 | solution.py:54
  199.0 2.9 fusion.76
  209.7 2.9 fusion.76
  220.4 2.9 fusion.76
  231.1 2.9 fusion.76
  241.8 2.9 fusion.76
  252.5 2.9 fusion.76
  263.2 2.9 fusion.76
  273.9 2.9 fusion.76
  280.7 13.8 %maximum_bitcast_fusion = bf16[2,1,1,128,128,256]{5,4,3,2,1,0:T(8,128)(2,1)} fusion(bf16[1,128,128,256]{3,2,1,0:T(8,128)(2,1)} %bitcast.87, bf16[1,128,128,256]{3,2,1,0:T(8,128)(2,1)} %bitcast.86), kind=kLoop, calls=%fused_computation.75 | loop fusion | flops 8388608 | bytes 33554432 | tf_op jit(solution)/shard_map/broadcast_in_dim | solution.py:84
  (169 shorter events, 158.8 us)
Async XLA Ops:
  0.0 65.0 %copy-start = (s32[2,8]{1,0:T(2,128)S(1)}, s32[2,8]{1,0:T(2,128)}, u32[]{:S(2)}) copy-start(s32[2,8]{1,0:T(2,128)} %param.13) | copy-start | bytes 196
  0.0 88.2 %copy-start.2 = (f32[128,2,1024]{2,1,0:T(2,128)S(1)}, f32[128,2,1024]{2,1,0:T(2,128)}, u32[]{:S(2)}) copy-start(f32[128,2,1024]{2,1,0:T(2,128)} %param.10) | copy-start | bytes 3145732
  0.0 64.2 %copy-start.5 = (s32[1,128]{1,0:T(1,128)S(1)}, s32[1,128]{1,0:T(1,128)}, u32[]{:S(2)}) copy-start(s32[1,128]{1,0:T(1,128)} %param.12) | copy-start | bytes 1540
  4.0 28.3 %collective-permute-start = (f32[128,2,1024]{2,1,0:T(2,128)S(1)}, f32[128,2,1024]{2,1,0:T(2,128)S(1)}, u32[]{:S(2)}, u32[]{:S(2)}) collective-permute-start(f32[128,2,1024]{2,1,0:T(2,128)S(1)} %broadcast_multiply_fusion), channel_id=1, source_target_pairs={{0,1},{1,2},{2,3},{3,0},{4,5},{5,6},{6,7},{7,4},{8,9},{9,10},{10,1... | collective-permute-start | bytes 3145736 | tf_op jit(solution)/shard_map/ppermute | solution.py:70
  32.3 31.8 %copy-start.3 = (f32[128,2,1024]{2,1,0:T(2,128)}, f32[128,2,1024]{2,1,0:T(2,128)S(1)}, u32[]{:S(2)}) copy-start(f32[128,2,1024]{2,1,0:T(2,128)S(1)} %collective-permute-done) | copy-start | bytes 3145732
  32.3 26.2 %collective-permute-start.1 = (f32[128,2,1024]{2,1,0:T(2,128)S(1)}, f32[128,2,1024]{2,1,0:T(2,128)}, u32[]{:S(2)}, u32[]{:S(2)}) collective-permute-start(f32[128,2,1024]{2,1,0:T(2,128)S(1)} %collective-permute-done), channel_id=1, source_target_pairs={{0,1},{1,2},{2,3},{3,0},{4,5},{5,6},{6,7},{7,4},{8,9},{9,10},{10,1... | collective-permute-start | bytes 3145736 | tf_op jit(solution)/shard_map/ppermute | solution.py:70
  58.6 25.6 %collective-permute-start.2 = (f32[128,2,1024]{2,1,0:T(2,128)}, f32[128,2,1024]{2,1,0:T(2,128)}, u32[]{:S(2)}, u32[]{:S(2)}) collective-permute-start(f32[128,2,1024]{2,1,0:T(2,128)} %collective-permute-done.1), channel_id=1, source_target_pairs={{0,1},{1,2},{2,3},{3,0},{4,5},{5,6},{6,7},{7,4},{8,9},{9,10},{10,1... | collective-permute-start | bytes 3145736 | tf_op jit(solution)/shard_map/ppermute | solution.py:70
  64.7 29.1 %collective-permute-start.3 = (f32[128,2,1024]{2,1,0:T(2,128)S(1)}, f32[128,2,1024]{2,1,0:T(2,128)S(1)}, u32[]{:S(2)}, u32[]{:S(2)}) collective-permute-start(f32[128,2,1024]{2,1,0:T(2,128)S(1)} %broadcast_select_fusion), channel_id=1, source_target_pairs={{0,4},{4,8},{8,12},{12,16},{16,20},{20,24},{24,28},{28,0},{1,5},{5... | collective-permute-start | bytes 3145736 | tf_op jit(solution)/shard_map/ppermute | solution.py:14
  66.8 24.6 %copy-start.4 = (f32[128,2,1024]{2,1,0:T(2,128)S(1)}, f32[128,2,1024]{2,1,0:T(2,128)}, u32[]{:S(2)}) copy-start(f32[128,2,1024]{2,1,0:T(2,128)} %copy-done.3) | copy-start | bytes 3145732
  280.7 13.8 %copy-start.1 = (s32[2,8]{1,0:T(2,128)S(1)}, s32[2,8]{1,0:T(2,128)}, u32[]{:S(2)}) copy-start(s32[2,8]{1,0:T(2,128)} %param.13) | copy-start | bytes 196
